TPU v7x, 512 devices: a whole 4x8x8 slice. The times are simulated.
512 devices in a mesh: region: 32 (over x, z), batch: 16 (over y, core).
Axes of the slice: x: 4, y: 8, z: 8, core: 2. Of those that a mesh axis runs over, the one named last changes fastest.
Arguments:
- basis_values: bfloat16 [128, 2, 4096, 512], P('region', None, 'batch'), may hold values from -6 to 6
- dens_tiles: bfloat16 [128, 512, 512], P('region', 'batch'), may hold values from -0.005859375 to 0.005859375
- region_tiles: int32 [128, 3], replicated, may hold values from 0 to 127, as said below
- point_counts: int32 [128, 16], P('region', 'batch'), may hold values from 64 to 256, as said below
- point_weights: float32 [128, 4096], P('region', 'batch'), may hold values from 0.0078125 to 0.03125
Outputs:
- xc_tiles: float32 [128, 512, 512], P('region', 'batch')
Inputs may be any that keep to these rules, and one draw needn't show every extreme that they name: `region_tiles`: tile t is stored on index t // 4 of region. Regions 4 * i to 4 * i + 3 lie on index i; among their 12 entries no owner index holds more than 1 and some owner holds exactly 1, on every index; the entries of one owner on one index are different tiles. `point_counts`: every region has at least one batch with all 256 points live.
All inputs are finite; a program needn't handle non-finite values.
Results may differ from a plain program's by a relative error of at most 0.004.
Values may be sent and summed in bfloat16 or wider, within the bound.
A program may use at most 64 MiB of HBM per device.

v0:
```python
import jax
import jax.numpy as jnp
from jax import lax
from jax.sharding import PartitionSpec as P

SLATER = 0.9847450218426964


def potential(density):
    return -SLATER * density * jnp.power(density * density + 1.0, -1.0 / 3.0)


def shards(basis_values, dens_tiles, region_tiles, point_counts, point_weights):
    owner_count = lax.axis_size("region")
    batch_count = lax.axis_size("batch")
    my_index = lax.axis_index("region")
    region_local = basis_values.shape[0]
    point_local = basis_values.shape[2]
    tile_local = dens_tiles.shape[0]
    row_count = dens_tiles.shape[1]
    block_width = dens_tiles.shape[2]
    requests = 3 * region_local
    slot_total = (requests + owner_count - 1) // owner_count
    table = region_tiles.reshape(owner_count, requests)
    owners = table // tile_local
    local_ids = table % tile_local
    order = jnp.arange(requests, dtype=jnp.int32)
    earlier = (owners[:, :, None] == owners[:, None, :]) & (
        order[None, None, :] < order[None, :, None]
    )
    ranks = jnp.sum(earlier.astype(jnp.int32), axis=2)
    slot_ids = jnp.arange(slot_total, dtype=jnp.int32)
    tile_ids = jnp.arange(tile_local, dtype=jnp.int32)
    chosen = (
        (owners == my_index)[:, :, None, None]
        & (ranks[:, :, None, None] == slot_ids[None, None, :, None])
        & (local_ids[:, :, None, None] == tile_ids[None, None, None, :])
    )
    selector = jnp.sum(chosen.astype(jnp.float32), axis=1)
    my_owners = lax.dynamic_index_in_dim(owners, my_index, 0, keepdims=False)
    my_ranks = lax.dynamic_index_in_dim(ranks, my_index, 0, keepdims=False)
    outgoing = jnp.einsum(
        "dct,trb->dcrb",
        selector.astype(jnp.bfloat16),
        dens_tiles,
        preferred_element_type=jnp.float32,
    ).astype(jnp.bfloat16)
    incoming = lax.all_to_all(outgoing, "region", split_axis=0, concat_axis=0, tiled=True)
    flat = incoming.reshape(owner_count * slot_total, row_count, block_width)
    fetched = jnp.take(flat, my_owners * slot_total + my_ranks, axis=0)
    piece = lax.all_gather(fetched, "batch", axis=1, tiled=True)
    count = piece.shape[1]
    shaped = piece.reshape(region_local, 3, count, block_width)
    left_aa = jnp.einsum(
        "rpc,rcb->rpb", basis_values[:, 0], shaped[:, 0], preferred_element_type=jnp.float32
    )
    left_ab = jnp.einsum(
        "rpc,rcb->rpb", basis_values[:, 0], shaped[:, 1], preferred_element_type=jnp.float32
    )
    left_bb = jnp.einsum(
        "rpc,rcb->rpb", basis_values[:, 1], shaped[:, 2], preferred_element_type=jnp.float32
    )
    left_aa, left_ab, left_bb = (left_aa, left_ab, left_bb)
    phi_a = basis_values[:, 0]
    phi_b = basis_values[:, 1]
    density = (
        jnp.sum(phi_a * left_aa, axis=-1)
        + 2.0 * jnp.sum(phi_b * left_ab, axis=-1)
        + jnp.sum(phi_b * left_bb, axis=-1)
    )
    live = jnp.arange(point_local, dtype=jnp.int32)[None, :] < point_counts
    scale = jnp.where(live, point_weights * potential(density), 0.0)
    scaled_a = (scale[:, :, None] * phi_a).astype(jnp.bfloat16)
    scaled_b = (scale[:, :, None] * phi_b).astype(jnp.bfloat16)
    first = jnp.einsum("rpc,rpb->crb", phi_a, scaled_a, preferred_element_type=jnp.float32)
    second = jnp.einsum("rpc,rpb->crb", phi_a, scaled_b, preferred_element_type=jnp.float32)
    third = jnp.einsum("rpc,rpb->crb", phi_b, scaled_b, preferred_element_type=jnp.float32)
    partial_pairs = jnp.stack([first, second, third], axis=2).reshape(
        block_width, requests, block_width
    )
    partial_pairs = partial_pairs.astype(jnp.bfloat16).reshape(
        batch_count, row_count, requests, block_width
    )
    received = lax.all_to_all(partial_pairs, "batch", split_axis=0, concat_axis=0, tiled=True)
    pairs = jnp.sum(received.astype(jnp.float32), axis=0)
    placement = (
        (my_owners[:, None, None] == jnp.arange(owner_count, dtype=jnp.int32)[None, :, None])
        & (my_ranks[:, None, None] == slot_ids[None, None, :])
    ).astype(jnp.float32)
    outgoing_sums = jnp.einsum("jdc,rjb->dcrb", placement, pairs, precision=lax.Precision.HIGHEST)
    returned = lax.all_to_all(outgoing_sums, "region", split_axis=0, concat_axis=0, tiled=True)
    return jnp.einsum("dct,dcrb->trb", selector, returned, precision=lax.Precision.HIGHEST)


def solution(mesh):
    return jax.shard_map(
        shards,
        mesh=mesh,
        in_specs=(
            P("region", None, "batch", None),
            P("region", "batch", None),
            P(),
            P("region", "batch"),
            P("region", "batch"),
        ),
        out_specs=P("region", "batch", None),
        check_vma=False,
    )
```

profile of v0, /device:TPU:1, one launch (start us, length us, event | category | flops | bytes accessed | tf_op | source)
XLA Modules:
  0.0 331.1 jit_solution(2894611914320594194)
XLA Ops:
  6.5 0.0 copy-start
  6.5 0.8 copy.81
  7.4 0.1 reshape.254
  7.4 0.1 copy.82
  7.6 0.1 convert_reduce_fusion.1
  7.7 0.0 copy-done
  7.7 0.5 fusion.14
  8.2 1.6 copy.88
  9.8 0.0 copy-start.1
  9.8 13.8 %all-to-all-start = ((bf16[32,1,32,512]{3,2,1,0:T(8,128)(2,1)}), bf16[32,1,32,512]{3,2,1,0:T(8,128)(2,1)S(1)}, u32[]{:S(2)}, u32[]{:S(2)}) async-start(bf16[32,1,32,512]{3,2,1,0:T(8,128)(2,1)} %copy.88), calls=%async_computation | async-start | bytes 2097152 | tf_op jit(solution)/shard_map/all_to_all | solution.py:48
  23.6 0.0 all-gather.2.cloned.1.call-start
  23.7 0.2 dynamic-slice_reduce_fusion
  24.0 24.3 %all-to-all-done = bf16[32,1,32,512]{3,2,1,0:T(8,128)(2,1)S(1)} async-done(((bf16[32,1,32,512]{3,2,1,0:T(8,128)(2,1)}), bf16[32,1,32,512]{3,2,1,0:T(8,128)(2,1)S(1)}, u32[]{:S(2)}, u32[]{:S(2)}) %all-to-all-start) | async-done | bytes 1048608 | tf_op jit(solution)/shard_map/all_to_all | solution.py:48
  48.3 1.4 gather_fusion
  49.6 1.9 broadcast_select_fusion
  51.5 0.0 all-gather.2.cloned.1.call-update
  51.5 49.9 %all-gather.2.cloned.1.call-done = bf16[12,512,512]{2,1,0:T(8,128)(2,1)} async-done(((bf16[12,32,512]{2,1,0:T(8,128)(2,1)}), bf16[12,512,512]{2,1,0:T(8,128)(2,1)}) %all-gather.2.cloned.1.call-update) | async-done | bytes 6291472 | tf_op jit(solution)/shard_map/all_gather | solution.py:51
  101.5 0.0 copy-done.1
  101.5 0.0 copy-start.4
  101.5 2.5 fusion.2
  104.0 0.9 copy-done.4
  104.9 0.8 fusion
  105.7 0.0 copy-start.2
  105.7 0.0 copy-start.3
  105.7 0.8 fusion.3
  106.5 0.0 copy-done.2
  106.5 0.0 copy-done.3
  106.5 0.1 multiply_select_fusion
  106.6 0.9 convert_bitcast_fusion.1
  107.5 0.9 convert_bitcast_fusion
  108.4 0.9 convert_bitcast_fusion.2
  109.4 0.8 pad_maximum_fusion
  110.2 0.4 copy.99
  110.6 1.1 copy.100
  111.8 145.4 %all_to_all.15 = bf16[16,32,12,512]{3,1,2,0:T(8,128)(2,1)S(1)} all-to-all(bf16[16,32,12,512]{3,1,2,0:T(8,128)(2,1)S(1)} %copy.100), channel_id=1, replica_groups=mesh['region'=32,'batch'=16] {'batch'}, dimensions={0} | all-to-all | bytes 12582912 | tf_op jit(solution)/shard_map/all_to_all | solution.py:84
  257.1 1.3 convert_reduce_fusion
  258.4 1.4 convolution_bitcast_fusion
  259.8 1.2 copy.103
  261.0 60.3 %all_to_all.16 = f32[32,1,32,512]{3,2,1,0:T(8,128)S(1)} all-to-all(f32[32,1,32,512]{3,2,1,0:T(8,128)S(1)} %copy.103), channel_id=1, replica_groups=mesh['region'=32,'batch'=16] {'region'}, dimensions={0} | all-to-all | bytes 4194304 | tf_op jit(solution)/shard_map/all_to_all | solution.py:91
  321.3 2.2 fusion.8
  323.5 0.8 copy.105
  (7 shorter events, 0.1 us)
Async XLA Ops:
  6.5 1.2 copy-start
  9.8 91.7 %copy-start.1 = (bf16[4,2,256,512]{3,2,1,0:T(8,128)(2,1)S(1)}, bf16[4,2,256,512]{3,2,1,0:T(8,128)(2,1)}, u32[]{:S(2)}) copy-start(bf16[4,2,256,512]{3,2,1,0:T(8,128)(2,1)} %param.5) | copy-start | bytes 6291460
  9.8 38.5 %all-to-all-start = ((bf16[32,1,32,512]{3,2,1,0:T(8,128)(2,1)}), bf16[32,1,32,512]{3,2,1,0:T(8,128)(2,1)S(1)}, u32[]{:S(2)}, u32[]{:S(2)}) async-start(bf16[32,1,32,512]{3,2,1,0:T(8,128)(2,1)} %copy.88), calls=%async_computation | async-start | bytes 2097152 | tf_op jit(solution)/shard_map/all_to_all | solution.py:48
  23.6 77.8 %all-gather.2.cloned.1.call-start = ((), (), s32[]{:S(2)}) async-start(), calls=%async_computation.3 | async-start | bytes 6684672 | tf_op jit(solution)/shard_map/all_gather | solution.py:51
  101.5 3.4 %copy-start.4 = (bf16[12,512,512]{2,1,0:T(8,128)(2,1)S(1)}, bf16[12,512,512]{2,1,0:T(8,128)(2,1)}, u32[]{:S(2)}) copy-start(bf16[12,512,512]{2,1,0:T(8,128)(2,1)} %all-gather.2.cloned.1.call-done) | copy-start | bytes 18874372
  105.7 0.8 copy-start.2
  105.7 0.8 copy-start.3
Sparse Core Ops, SparseCore 0:
  51.6 49.7 all-gather.1
where the time goes:
time: 331 us
  blocking collectives  206 us (62%)
  waiting for transfers between devices  74.3 us (22%)
  starting transfers between devices  13.9 us (4%)
  between operations  13.6 us (4%)
  matrix products  11 us (3%)
  local copies, waits for them, and re-layouts  8.33 us (3%)
  other arithmetic  4.43 us (1%)
    all_to_all x1, blocking collectives, shards(): lax.all_to_all(partial_pairs, 'batch', split_axis=0, concat_axis=0, tiled...  145 us
    all_to_all x1, blocking collectives, shards(): lax.all_to_all(outgoing_sums, 'region', split_axis=0, concat_axis=0, tile...  60.3 us
    all_gather x1, waiting for transfers between devices, shards(): piece = lax.all_gather(fetched, 'batch', axis=1, tiled=True)  49.9 us
    all_to_all x1, waiting for transfers between devices, shards(): lax.all_to_all(outgoing, 'region', split_axis=0, concat_axis=0, tiled=True)  24.3 us
    all_to_all x1, starting transfers between devices, shards(): lax.all_to_all(outgoing, 'region', split_axis=0, concat_axis=0, tiled=True)  13.8 us
  transfers between devices with their start and end apart: 2, of which 2 were waited for; matrix products, arithmetic and copies ran while one was open for 0% of the time, Pallas kernels for 0%

commit v1 on v0

--- a/solution.py
+++ b/solution.py
@@ -48,7 +48,14 @@
     incoming = lax.all_to_all(outgoing, "region", split_axis=0, concat_axis=0, tiled=True)
     flat = incoming.reshape(owner_count * slot_total, row_count, block_width)
     fetched = jnp.take(flat, my_owners * slot_total + my_ranks, axis=0)
-    piece = lax.all_gather(fetched, "batch", axis=1, tiled=True)
+    ring = [fetched]
+    for hop in range(15):
+        ring.append(lax.ppermute(ring[-1], "batch", [(dev, (dev + 1) % 16) for dev in range(16)]))
+    piece = jnp.roll(
+        jnp.concatenate(ring[::-1], axis=1),
+        (lax.axis_index("batch") + 1) * ring[0].shape[1],
+        axis=1,
+    )
     count = piece.shape[1]
     shaped = piece.reshape(region_local, 3, count, block_width)
     left_aa = jnp.einsum(

time: 331 us -> 434 us (1.31)
  waiting for transfers between devices: 74.3 us -> 129 us
  local copies, waits for them, and re-layouts: 8.33 us -> 46.8 us
  starting transfers between devices: 13.9 us -> 33.2 us
  between operations: 13.6 us -> 0.28 us
    ppermute x0 -> x15, waiting for transfers between devices: none -> 105 us  [shards(): lax.ppermute(ring[-1], 'batch', [(dev, (dev + 1) % 16) for dev in range(1...]
    all_gather x1 -> x0, waiting for transfers between devices: 49.9 us -> none  [shards(): piece = lax.all_gather(fetched, 'batch', axis=1, tiled=True)]
    unnamed x11 -> x61, local copies, waits for them, and re-layouts: 1.72 us -> 37.4 us
    ppermute x0 -> x15, starting transfers between devices: none -> 19.5 us  [shards(): lax.ppermute(ring[-1], 'batch', [(dev, (dev + 1) % 16) for dev in range(1...]
    all_to_all x1, blocking collectives: 145 us -> 155 us  [shards(): lax.all_to_all(partial_pairs, 'batch', split_axis=0, concat_axis=0, tiled...]
    all_to_all x1, blocking collectives: 60.3 us -> 55.1 us  [shards(): lax.all_to_all(outgoing_sums, 'region', split_axis=0, concat_axis=0, tile...]
  transfers between devices with their start and end apart: 2 -> 16, of which waited for: 2 -> 16; matrix products, arithmetic and copies ran while one was open for 0% -> 0% of each run, Pallas kernels for 0% -> 0%
where the time goes in v1:
time: 434 us
  blocking collectives  210 us (48%)
  waiting for transfers between devices  129 us (30%)
  local copies, waits for them, and re-layouts  46.8 us (11%)
  starting transfers between devices  33.2 us (8%)
  matrix products  9.31 us (2%)
  other arithmetic  4.45 us (1%)
    all_to_all x1, blocking collectives, shards(): lax.all_to_all(partial_pairs, 'batch', split_axis=0, concat_axis=0, tiled...  155 us
    ppermute x15, waiting for transfers between devices, shards(): lax.ppermute(ring[-1], 'batch', [(dev, (dev + 1) % 16) for dev in range(1...  105 us
    all_to_all x1, blocking collectives, shards(): lax.all_to_all(outgoing_sums, 'region', split_axis=0, concat_axis=0, tile...  55.1 us
    unnamed x61, local copies, waits for them, and re-layouts  37.4 us
    all_to_all x1, waiting for transfers between devices, shards(): lax.all_to_all(outgoing, 'region', split_axis=0, concat_axis=0, tiled=True)  24.4 us
    ppermute x15, starting transfers between devices, shards(): lax.ppermute(ring[-1], 'batch', [(dev, (dev + 1) % 16) for dev in range(1...  19.5 us
    all_to_all x1, starting transfers between devices, shards(): lax.all_to_all(outgoing, 'region', split_axis=0, concat_axis=0, tiled=True)  13.7 us
  transfers between devices with their start and end apart: 16, of which 16 were waited for; matrix products, arithmetic and copies ran while one was open for 0% of the time, Pallas kernels for 0%

profile of v1, /device:TPU:1, one launch (start us, length us, event | category | flops | bytes accessed | tf_op | source)
XLA Modules:
  0.0 433.6 jit_solution(10479765883469565073)
XLA Ops:
  1.7 1.5 copy.85
  3.2 13.7 %all-to-all-start = ((bf16[32,1,32,512]{3,2,1,0:T(8,128)(2,1)}), bf16[32,1,32,512]{3,2,1,0:T(8,128)(2,1)S(1)}, u32[]{:S(2)}, u32[]{:S(2)}) async-start(bf16[32,1,32,512]{3,2,1,0:T(8,128)(2,1)} %copy.85), calls=%async_computation | async-start | bytes 2097152 | tf_op jit(solution)/shard_map/all_to_all | solution.py:48
  17.2 24.4 %all-to-all-done = bf16[32,1,32,512]{3,2,1,0:T(8,128)(2,1)S(1)} async-done(((bf16[32,1,32,512]{3,2,1,0:T(8,128)(2,1)}), bf16[32,1,32,512]{3,2,1,0:T(8,128)(2,1)S(1)}, u32[]{:S(2)}, u32[]{:S(2)}) %all-to-all-start) | async-done | bytes 1048608 | tf_op jit(solution)/shard_map/all_to_all | solution.py:48
  42.3 6.2 %collective-permute-start = (bf16[12,32,512]{2,1,0:T(8,128)(2,1)S(1)}, bf16[12,32,512]{2,1,0:T(8,128)(2,1)S(1)}, u32[]{:S(2)}, u32[]{:S(2)}) collective-permute-start(bf16[12,32,512]{2,1,0:T(8,128)(2,1)S(1)} %broadcast_select_fusion), channel_id=1, source_target_pairs={{0,1},{1,2},{2,3},{3,4},{4,5},{5,6},{6,7},{7,8},{8,9},{9,10},{10,1... | collective-permute-start | bytes 1179656 | tf_op jit(solution)/shard_map/ppermute | solution.py:53
  48.4 4.7 %collective-permute-done = bf16[12,32,512]{2,1,0:T(8,128)(2,1)S(1)} collective-permute-done((bf16[12,32,512]{2,1,0:T(8,128)(2,1)S(1)}, bf16[12,32,512]{2,1,0:T(8,128)(2,1)S(1)}, u32[]{:S(2)}, u32[]{:S(2)}) %collective-permute-start) | collective-permute-done | bytes 393248 | tf_op jit(solution)/shard_map/ppermute | solution.py:53
  53.2 2.5 collective-permute-start.1
  55.6 4.7 %collective-permute-done.1 = bf16[12,32,512]{2,1,0:T(8,128)(2,1)S(1)} collective-permute-done((bf16[12,32,512]{2,1,0:T(8,128)(2,1)S(1)}, bf16[12,32,512]{2,1,0:T(8,128)(2,1)S(1)}, u32[]{:S(2)}, u32[]{:S(2)}) %collective-permute-start.1) | collective-permute-done | bytes 393248 | tf_op jit(solution)/shard_map/ppermute | solution.py:53
  60.4 2.5 collective-permute-start.2
  62.8 4.7 %collective-permute-done.2 = bf16[12,32,512]{2,1,0:T(8,128)(2,1)S(1)} collective-permute-done((bf16[12,32,512]{2,1,0:T(8,128)(2,1)S(1)}, bf16[12,32,512]{2,1,0:T(8,128)(2,1)S(1)}, u32[]{:S(2)}, u32[]{:S(2)}) %collective-permute-start.2) | collective-permute-done | bytes 393248 | tf_op jit(solution)/shard_map/ppermute | solution.py:53
  67.6 2.5 collective-permute-start.3
  70.0 4.7 %collective-permute-done.3 = bf16[12,32,512]{2,1,0:T(8,128)(2,1)S(1)} collective-permute-done((bf16[12,32,512]{2,1,0:T(8,128)(2,1)S(1)}, bf16[12,32,512]{2,1,0:T(8,128)(2,1)S(1)}, u32[]{:S(2)}, u32[]{:S(2)}) %collective-permute-start.3) | collective-permute-done | bytes 393248 | tf_op jit(solution)/shard_map/ppermute | solution.py:53
  74.8 2.5 collective-permute-start.4
  77.2 4.9 %collective-permute-done.4 = bf16[12,32,512]{2,1,0:T(8,128)(2,1)S(1)} collective-permute-done((bf16[12,32,512]{2,1,0:T(8,128)(2,1)S(1)}, bf16[12,32,512]{2,1,0:T(8,128)(2,1)S(1)}, u32[]{:S(2)}, u32[]{:S(2)}) %collective-permute-start.4) | collective-permute-done | bytes 393248 | tf_op jit(solution)/shard_map/ppermute | solution.py:53
  82.1 2.3 collective-permute-start.5
  84.4 6.1 %collective-permute-done.5 = bf16[12,32,512]{2,1,0:T(8,128)(2,1)S(1)} collective-permute-done((bf16[12,32,512]{2,1,0:T(8,128)(2,1)S(1)}, bf16[12,32,512]{2,1,0:T(8,128)(2,1)S(1)}, u32[]{:S(2)}, u32[]{:S(2)}) %collective-permute-start.5) | collective-permute-done | bytes 393248 | tf_op jit(solution)/shard_map/ppermute | solution.py:53
  90.5 1.1 collective-permute-start.6
  91.7 7.3 %collective-permute-done.6 = bf16[12,32,512]{2,1,0:T(8,128)(2,1)S(1)} collective-permute-done((bf16[12,32,512]{2,1,0:T(8,128)(2,1)S(1)}, bf16[12,32,512]{2,1,0:T(8,128)(2,1)S(1)}, u32[]{:S(2)}, u32[]{:S(2)}) %collective-permute-start.6) | collective-permute-done | bytes 393248 | tf_op jit(solution)/shard_map/ppermute | solution.py:53
  99.0 8.4 %collective-permute-done.7 = bf16[12,32,512]{2,1,0:T(8,128)(2,1)S(1)} collective-permute-done((bf16[12,32,512]{2,1,0:T(8,128)(2,1)S(1)}, bf16[12,32,512]{2,1,0:T(8,128)(2,1)S(1)}, u32[]{:S(2)}, u32[]{:S(2)}) %collective-permute-start.7) | collective-permute-done | bytes 393248 | tf_op jit(solution)/shard_map/ppermute | solution.py:53
  107.4 8.4 %collective-permute-done.8 = bf16[12,32,512]{2,1,0:T(8,128)(2,1)S(1)} collective-permute-done((bf16[12,32,512]{2,1,0:T(8,128)(2,1)S(1)}, bf16[12,32,512]{2,1,0:T(8,128)(2,1)S(1)}, u32[]{:S(2)}, u32[]{:S(2)}) %collective-permute-start.8) | collective-permute-done | bytes 393248 | tf_op jit(solution)/shard_map/ppermute | solution.py:53
  116.6 8.4 %collective-permute-done.9 = bf16[12,32,512]{2,1,0:T(8,128)(2,1)S(1)} collective-permute-done((bf16[12,32,512]{2,1,0:T(8,128)(2,1)S(1)}, bf16[12,32,512]{2,1,0:T(8,128)(2,1)S(1)}, u32[]{:S(2)}, u32[]{:S(2)}) %collective-permute-start.9) | collective-permute-done | bytes 393248 | tf_op jit(solution)/shard_map/ppermute | solution.py:53
  125.7 8.4 %collective-permute-done.10 = bf16[12,32,512]{2,1,0:T(8,128)(2,1)S(1)} collective-permute-done((bf16[12,32,512]{2,1,0:T(8,128)(2,1)S(1)}, bf16[12,32,512]{2,1,0:T(8,128)(2,1)S(1)}, u32[]{:S(2)}, u32[]{:S(2)}) %collective-permute-start.10) | collective-permute-done | bytes 393248 | tf_op jit(solution)/shard_map/ppermute | solution.py:53
  134.9 8.4 %collective-permute-done.11 = bf16[12,32,512]{2,1,0:T(8,128)(2,1)S(1)} collective-permute-done((bf16[12,32,512]{2,1,0:T(8,128)(2,1)S(1)}, bf16[12,32,512]{2,1,0:T(8,128)(2,1)S(1)}, u32[]{:S(2)}, u32[]{:S(2)}) %collective-permute-start.11) | collective-permute-done | bytes 393248 | tf_op jit(solution)/shard_map/ppermute | solution.py:53
  144.1 8.4 %collective-permute-done.12 = bf16[12,32,512]{2,1,0:T(8,128)(2,1)S(1)} collective-permute-done((bf16[12,32,512]{2,1,0:T(8,128)(2,1)S(1)}, bf16[12,32,512]{2,1,0:T(8,128)(2,1)S(1)}, u32[]{:S(2)}, u32[]{:S(2)}) %collective-permute-start.12) | collective-permute-done | bytes 393248 | tf_op jit(solution)/shard_map/ppermute | solution.py:53
  153.2 8.5 %collective-permute-done.13 = bf16[12,32,512]{2,1,0:T(8,128)(2,1)} collective-permute-done((bf16[12,32,512]{2,1,0:T(8,128)(2,1)S(1)}, bf16[12,32,512]{2,1,0:T(8,128)(2,1)}, u32[]{:S(2)}, u32[]{:S(2)}) %collective-permute-start.13) | collective-permute-done | bytes 393248 | tf_op jit(solution)/shard_map/ppermute | solution.py:53
  161.8 8.7 %collective-permute-done.14 = bf16[12,32,512]{2,1,0:T(8,128)(2,1)} collective-permute-done((bf16[12,32,512]{2,1,0:T(8,128)(2,1)}, bf16[12,32,512]{2,1,0:T(8,128)(2,1)}, u32[]{:S(2)}, u32[]{:S(2)}) %collective-permute-start.14) | collective-permute-done | bytes 393248 | tf_op jit(solution)/shard_map/ppermute | solution.py:53
  170.5 1.8 constant_dynamic-update-slice_fusion.31
  172.3 1.8 constant_dynamic-update-slice_fusion.30
  174.1 1.8 constant_dynamic-update-slice_fusion.29
  175.8 1.8 constant_dynamic-update-slice_fusion.28
  177.6 1.8 constant_dynamic-update-slice_fusion.27
  179.4 1.8 constant_dynamic-update-slice_fusion.26
  181.2 1.8 constant_dynamic-update-slice_fusion.25
  189.3 0.9 constant_dynamic-update-slice_fusion.16
  190.2 1.9 constant_dynamic-update-slice_fusion.15
  192.1 1.8 constant_dynamic-update-slice_fusion.14
  204.2 0.9 constant_dynamic-update-slice_fusion
  205.1 3.6 constant_dynamic-slice_fusion
  211.2 1.0 convert_bitcast_fusion.1
  212.1 0.9 convert_bitcast_fusion
  213.1 0.9 convert_bitcast_fusion.2
  214.0 0.8 pad_maximum_fusion
  215.2 1.1 copy.97
  216.4 155.1 %all_to_all.15 = bf16[16,32,12,512]{3,1,2,0:T(8,128)(2,1)S(1)} all-to-all(bf16[16,32,12,512]{3,1,2,0:T(8,128)(2,1)S(1)} %copy.97), channel_id=1, replica_groups=mesh['region'=32,'batch'=16] {'batch'}, dimensions={0} | all-to-all | bytes 12582912 | tf_op jit(solution)/shard_map/all_to_all | solution.py:91
  371.5 1.3 convert_reduce_fusion
  372.8 1.4 convolution_bitcast_fusion
  374.2 1.2 copy.100
  375.4 55.1 %all_to_all.16 = f32[32,1,32,512]{3,2,1,0:T(8,128)S(1)} all-to-all(f32[32,1,32,512]{3,2,1,0:T(8,128)S(1)} %copy.100), channel_id=1, replica_groups=mesh['region'=32,'batch'=16] {'region'}, dimensions={0} | all-to-all | bytes 4194304 | tf_op jit(solution)/shard_map/all_to_all | solution.py:98
  430.6 2.2 fusion.8
  (80 shorter events, 26.7 us)
Async XLA Ops:
  0.0 1.2 copy-start
  3.2 38.3 %all-to-all-start = ((bf16[32,1,32,512]{3,2,1,0:T(8,128)(2,1)}), bf16[32,1,32,512]{3,2,1,0:T(8,128)(2,1)S(1)}, u32[]{:S(2)}, u32[]{:S(2)}) async-start(bf16[32,1,32,512]{3,2,1,0:T(8,128)(2,1)} %copy.85), calls=%async_computation | async-start | bytes 2097152 | tf_op jit(solution)/shard_map/all_to_all | solution.py:48
  42.3 10.9 %collective-permute-start = (bf16[12,32,512]{2,1,0:T(8,128)(2,1)S(1)}, bf16[12,32,512]{2,1,0:T(8,128)(2,1)S(1)}, u32[]{:S(2)}, u32[]{:S(2)}) collective-permute-start(bf16[12,32,512]{2,1,0:T(8,128)(2,1)S(1)} %broadcast_select_fusion), channel_id=1, source_target_pairs={{0,1},{1,2},{2,3},{3,4},{4,5},{5,6},{6,7},{7,8},{8,9},{9,10},{10,1... | collective-permute-start | bytes 1179656 | tf_op jit(solution)/shard_map/ppermute | solution.py:53
  53.2 7.2 %collective-permute-start.1 = (bf16[12,32,512]{2,1,0:T(8,128)(2,1)S(1)}, bf16[12,32,512]{2,1,0:T(8,128)(2,1)S(1)}, u32[]{:S(2)}, u32[]{:S(2)}) collective-permute-start(bf16[12,32,512]{2,1,0:T(8,128)(2,1)S(1)} %collective-permute-done), channel_id=1, source_target_pairs={{0,1},{1,2},{2,3},{3,4},{4,5},{5,6},{6,7},{7,8},{8,9},{9,10},{10,1... | collective-permute-start | bytes 1179656 | tf_op jit(solution)/shard_map/ppermute | solution.py:53
  60.4 7.2 %collective-permute-start.2 = (bf16[12,32,512]{2,1,0:T(8,128)(2,1)S(1)}, bf16[12,32,512]{2,1,0:T(8,128)(2,1)S(1)}, u32[]{:S(2)}, u32[]{:S(2)}) collective-permute-start(bf16[12,32,512]{2,1,0:T(8,128)(2,1)S(1)} %collective-permute-done.1), channel_id=1, source_target_pairs={{0,1},{1,2},{2,3},{3,4},{4,5},{5,6},{6,7},{7,8},{8,9},{9,10},{10,1... | collective-permute-start | bytes 1179656 | tf_op jit(solution)/shard_map/ppermute | solution.py:53
  67.6 7.2 %collective-permute-start.3 = (bf16[12,32,512]{2,1,0:T(8,128)(2,1)S(1)}, bf16[12,32,512]{2,1,0:T(8,128)(2,1)S(1)}, u32[]{:S(2)}, u32[]{:S(2)}) collective-permute-start(bf16[12,32,512]{2,1,0:T(8,128)(2,1)S(1)} %collective-permute-done.2), channel_id=1, source_target_pairs={{0,1},{1,2},{2,3},{3,4},{4,5},{5,6},{6,7},{7,8},{8,9},{9,10},{10,1... | collective-permute-start | bytes 1179656 | tf_op jit(solution)/shard_map/ppermute | solution.py:53
  74.8 7.4 %collective-permute-start.4 = (bf16[12,32,512]{2,1,0:T(8,128)(2,1)S(1)}, bf16[12,32,512]{2,1,0:T(8,128)(2,1)S(1)}, u32[]{:S(2)}, u32[]{:S(2)}) collective-permute-start(bf16[12,32,512]{2,1,0:T(8,128)(2,1)S(1)} %collective-permute-done.3), channel_id=1, source_target_pairs={{0,1},{1,2},{2,3},{3,4},{4,5},{5,6},{6,7},{7,8},{8,9},{9,10},{10,1... | collective-permute-start | bytes 1179656 | tf_op jit(solution)/shard_map/ppermute | solution.py:53
  82.1 8.4 %collective-permute-start.5 = (bf16[12,32,512]{2,1,0:T(8,128)(2,1)S(1)}, bf16[12,32,512]{2,1,0:T(8,128)(2,1)S(1)}, u32[]{:S(2)}, u32[]{:S(2)}) collective-permute-start(bf16[12,32,512]{2,1,0:T(8,128)(2,1)S(1)} %collective-permute-done.4), channel_id=1, source_target_pairs={{0,1},{1,2},{2,3},{3,4},{4,5},{5,6},{6,7},{7,8},{8,9},{9,10},{10,1... | collective-permute-start | bytes 1179656 | tf_op jit(solution)/shard_map/ppermute | solution.py:53
  90.5 8.4 %collective-permute-start.6 = (bf16[12,32,512]{2,1,0:T(8,128)(2,1)S(1)}, bf16[12,32,512]{2,1,0:T(8,128)(2,1)S(1)}, u32[]{:S(2)}, u32[]{:S(2)}) collective-permute-start(bf16[12,32,512]{2,1,0:T(8,128)(2,1)S(1)} %collective-permute-done.5), channel_id=1, source_target_pairs={{0,1},{1,2},{2,3},{3,4},{4,5},{5,6},{6,7},{7,8},{8,9},{9,10},{10,1... | collective-permute-start | bytes 1179656 | tf_op jit(solution)/shard_map/ppermute | solution.py:53
  99.0 8.4 %collective-permute-start.7 = (bf16[12,32,512]{2,1,0:T(8,128)(2,1)S(1)}, bf16[12,32,512]{2,1,0:T(8,128)(2,1)S(1)}, u32[]{:S(2)}, u32[]{:S(2)}) collective-permute-start(bf16[12,32,512]{2,1,0:T(8,128)(2,1)S(1)} %collective-permute-done.6), channel_id=1, source_target_pairs={{0,1},{1,2},{2,3},{3,4},{4,5},{5,6},{6,7},{7,8},{8,9},{9,10},{10,1... | collective-permute-start | bytes 1179656 | tf_op jit(solution)/shard_map/ppermute | solution.py:53
  107.4 8.4 %collective-permute-start.8 = (bf16[12,32,512]{2,1,0:T(8,128)(2,1)S(1)}, bf16[12,32,512]{2,1,0:T(8,128)(2,1)S(1)}, u32[]{:S(2)}, u32[]{:S(2)}) collective-permute-start(bf16[12,32,512]{2,1,0:T(8,128)(2,1)S(1)} %collective-permute-done.7), channel_id=1, source_target_pairs={{0,1},{1,2},{2,3},{3,4},{4,5},{5,6},{6,7},{7,8},{8,9},{9,10},{10,1... | collective-permute-start | bytes 1179656 | tf_op jit(solution)/shard_map/ppermute | solution.py:53
  115.8 0.8 copy-start.3
  116.6 8.4 %collective-permute-start.9 = (bf16[12,32,512]{2,1,0:T(8,128)(2,1)S(1)}, bf16[12,32,512]{2,1,0:T(8,128)(2,1)S(1)}, u32[]{:S(2)}, u32[]{:S(2)}) collective-permute-start(bf16[12,32,512]{2,1,0:T(8,128)(2,1)S(1)} %collective-permute-done.8), channel_id=1, source_target_pairs={{0,1},{1,2},{2,3},{3,4},{4,5},{5,6},{6,7},{7,8},{8,9},{9,10},{10,1... | collective-permute-start | bytes 1179656 | tf_op jit(solution)/shard_map/ppermute | solution.py:53
  125.0 0.8 copy-start.5
  125.7 8.4 %collective-permute-start.10 = (bf16[12,32,512]{2,1,0:T(8,128)(2,1)S(1)}, bf16[12,32,512]{2,1,0:T(8,128)(2,1)S(1)}, u32[]{:S(2)}, u32[]{:S(2)}) collective-permute-start(bf16[12,32,512]{2,1,0:T(8,128)(2,1)S(1)} %collective-permute-done.9), channel_id=1, source_target_pairs={{0,1},{1,2},{2,3},{3,4},{4,5},{5,6},{6,7},{7,8},{8,9},{9,10},{10,1... | collective-permute-start | bytes 1179656 | tf_op jit(solution)/shard_map/ppermute | solution.py:53
  134.2 0.8 copy-start.7
  134.9 8.4 %collective-permute-start.11 = (bf16[12,32,512]{2,1,0:T(8,128)(2,1)S(1)}, bf16[12,32,512]{2,1,0:T(8,128)(2,1)S(1)}, u32[]{:S(2)}, u32[]{:S(2)}) collective-permute-start(bf16[12,32,512]{2,1,0:T(8,128)(2,1)S(1)} %collective-permute-done.10), channel_id=1, source_target_pairs={{0,1},{1,2},{2,3},{3,4},{4,5},{5,6},{6,7},{7,8},{8,9},{9,10},{10,1... | collective-permute-start | bytes 1179656 | tf_op jit(solution)/shard_map/ppermute | solution.py:53
  143.3 0.8 copy-start.9
  144.1 8.4 %collective-permute-start.12 = (bf16[12,32,512]{2,1,0:T(8,128)(2,1)S(1)}, bf16[12,32,512]{2,1,0:T(8,128)(2,1)S(1)}, u32[]{:S(2)}, u32[]{:S(2)}) collective-permute-start(bf16[12,32,512]{2,1,0:T(8,128)(2,1)S(1)} %collective-permute-done.11), channel_id=1, source_target_pairs={{0,1},{1,2},{2,3},{3,4},{4,5},{5,6},{6,7},{7,8},{8,9},{9,10},{10,1... | collective-permute-start | bytes 1179656 | tf_op jit(solution)/shard_map/ppermute | solution.py:53
  152.5 0.8 copy-start.11
  153.2 8.5 %collective-permute-start.13 = (bf16[12,32,512]{2,1,0:T(8,128)(2,1)S(1)}, bf16[12,32,512]{2,1,0:T(8,128)(2,1)}, u32[]{:S(2)}, u32[]{:S(2)}) collective-permute-start(bf16[12,32,512]{2,1,0:T(8,128)(2,1)S(1)} %collective-permute-done.12), channel_id=1, source_target_pairs={{0,1},{1,2},{2,3},{3,4},{4,5},{5,6},{6,7},{7,8},{8,9},{9,10},{10,1... | collective-permute-start | bytes 1179656 | tf_op jit(solution)/shard_map/ppermute | solution.py:53
  161.8 8.7 %collective-permute-start.14 = (bf16[12,32,512]{2,1,0:T(8,128)(2,1)}, bf16[12,32,512]{2,1,0:T(8,128)(2,1)}, u32[]{:S(2)}, u32[]{:S(2)}) collective-permute-start(bf16[12,32,512]{2,1,0:T(8,128)(2,1)} %collective-permute-done.13), channel_id=1, source_target_pairs={{0,1},{1,2},{2,3},{3,4},{4,5},{5,6},{6,7},{7,8},{8,9},{9,10},{10,1... | collective-permute-start | bytes 1179656 | tf_op jit(solution)/shard_map/ppermute | solution.py:53
  161.8 32.1 %copy-start.12 = (bf16[12,32,512]{2,1,0:T(8,128)(2,1)S(1)}, bf16[12,32,512]{2,1,0:T(8,128)(2,1)}, u32[]{:S(2)}) copy-start(bf16[12,32,512]{2,1,0:T(8,128)(2,1)} %copy-done.11) | copy-start | bytes 1179652
  161.8 32.9 %copy-start.10 = (bf16[12,32,512]{2,1,0:T(8,128)(2,1)S(1)}, bf16[12,32,512]{2,1,0:T(8,128)(2,1)}, u32[]{:S(2)}) copy-start(bf16[12,32,512]{2,1,0:T(8,128)(2,1)} %copy-done.9) | copy-start | bytes 1179652
  161.8 33.7 %copy-start.8 = (bf16[12,32,512]{2,1,0:T(8,128)(2,1)S(1)}, bf16[12,32,512]{2,1,0:T(8,128)(2,1)}, u32[]{:S(2)}) copy-start(bf16[12,32,512]{2,1,0:T(8,128)(2,1)} %copy-done.7) | copy-start | bytes 1179652
  161.8 34.5 %copy-start.6 = (bf16[12,32,512]{2,1,0:T(8,128)(2,1)S(1)}, bf16[12,32,512]{2,1,0:T(8,128)(2,1)}, u32[]{:S(2)}) copy-start(bf16[12,32,512]{2,1,0:T(8,128)(2,1)} %copy-done.5) | copy-start | bytes 1179652
  161.8 35.3 %copy-start.4 = (bf16[12,32,512]{2,1,0:T(8,128)(2,1)S(1)}, bf16[12,32,512]{2,1,0:T(8,128)(2,1)}, u32[]{:S(2)}) copy-start(bf16[12,32,512]{2,1,0:T(8,128)(2,1)} %copy-done.3) | copy-start | bytes 1179652
  190.2 18.5 %copy-start.2 = (bf16[4,2,256,512]{3,2,1,0:T(8,128)(2,1)S(1)}, bf16[4,2,256,512]{3,2,1,0:T(8,128)(2,1)}, u32[]{:S(2)}) copy-start(bf16[4,2,256,512]{3,2,1,0:T(8,128)(2,1)} %param.5) | copy-start | bytes 6291460
  208.6 2.4 copy-start.13
  208.7 2.4 copy-start.14
  216.4 217.2 %copy-start.1 = (bf16[4,32,512]{2,1,0:T(8,128)(2,1)S(1)}, bf16[4,32,512]{2,1,0:T(8,128)(2,1)}, u32[]{:S(2)}) copy-start(bf16[4,32,512]{2,1,0:T(8,128)(2,1)} %param.6) | copy-start | bytes 393220
